TPU v7x, 256 devices: a whole 4x4x8 slice. The times are simulated.
256 devices in a mesh: head: 8 (over x, core), seq: 32 (over z, y).
Axes of the slice: x: 4, y: 4, z: 8, core: 2. Of those that a mesh axis runs over, the one named last changes fastest.
Arguments:
- tokens: bfloat16 [4, 16, 2048], P(None, None, 'seq'), may hold values from -16 to 16
- attn_in_weight: bfloat16 [3, 2048, 2048], P(None, 'seq', 'head'), may hold values from -0.125 to 0.125
- attn_out_weight: bfloat16 [2048, 2048], P('head', 'seq'), may hold values from -0.125 to 0.125
- ffn_in_weight: bfloat16 [2, 2048, 8192], P(None, 'seq', 'head'), may hold values from -0.125 to 0.125
- ffn_out_weight: bfloat16 [8192, 2048], P('head', 'seq'), may hold values from -0.0625 to 0.0625
- cache_keys: bfloat16 [16, 16384, 2048], P(None, 'seq', 'head'), may hold values from -60 to 60
- cache_values: bfloat16 [16, 16384, 2048], P(None, 'seq', 'head'), may hold values from -10 to 10
- lengths: int32 [16], replicated, may hold values from 1 to 16384, as said below
Outputs:
- attn_branch: bfloat16 [4, 16, 2048], P(None, None, 'seq')
- mlp_branch: bfloat16 [4, 16, 2048], P(None, None, 'seq')
Inputs may be any that keep to these rules, and one draw needn't show every extreme that they name: `lengths`: some request has exactly 16384 filled positions.
All inputs are finite; a program needn't handle non-finite values.
Results may differ from a plain program's by a relative error of at most 0.013.
The roundings to bfloat16 on the way count: a program that leaves them out, or rounds other values in their place, can miss the bound.
Values may be sent and summed in bfloat16 or wider, within the bound.
No kernel may reach another device: no remote copies, remote signals or barrier semaphores. Data moves between devices by JAX's collectives and lax.ppermute only.
A program may use at most 64 MiB of HBM per device.

v0:
```python
import jax
import jax.numpy as jnp
from jax import lax
from jax.sharding import PartitionSpec as P

D = 2048
HD = 128


NORM_EPSILON = 1e-05
NEG_FILL = -1e30


def norm_rows(values):
    center = lax.psum(jnp.sum(values, axis=-1), "seq") / D
    deviate = values - center[:, None]
    spread = lax.psum(jnp.sum(deviate * deviate, axis=-1), "seq") / D
    return deviate * lax.rsqrt(spread + NORM_EPSILON)[:, None]


def rotate_pairs(values, positions):
    half_dim = values.shape[-1] // 2
    inverse_freq = 10000.0 ** (-2.0 * jnp.arange(half_dim, dtype=jnp.float32) / values.shape[-1])
    angles = positions.astype(jnp.float32)[:, None, None] * inverse_freq[None, None, :]
    cosine = jnp.cos(angles)
    sine = jnp.sin(angles)
    first_half = values[..., :half_dim]
    second_half = values[..., half_dim:]
    return jnp.concatenate(
        [first_half * cosine - second_half * sine, second_half * cosine + first_half * sine],
        axis=-1,
    )


def combine_parts(earlier, later_part):
    top_one, total_one, acc_one = earlier
    top_two, total_two, acc_two = later_part
    overall = jnp.maximum(top_one, top_two)
    factor_one = jnp.exp(top_one - overall)
    factor_two = jnp.exp(top_two - overall)
    return (
        overall,
        factor_one * total_one + factor_two * total_two,
        factor_one[..., None] * acc_one + factor_two[..., None] * acc_two,
    )


def per_device(
    tokens,
    attn_in_weight,
    attn_out_weight,
    ffn_in_weight,
    ffn_out_weight,
    cache_keys,
    cache_values,
    lengths,
):
    step_count, request_count, width_local = tokens.shape
    row_count = step_count * request_count
    inputs = tokens.reshape(row_count, width_local).astype(jnp.float32)
    normed = norm_rows(inputs).astype(jnp.bfloat16)
    partial_qkv = jnp.einsum(
        "nd,kde->kne", normed, attn_in_weight, preferred_element_type=jnp.float32
    )
    projected = lax.psum(partial_qkv, "seq")
    heads_local = attn_in_weight.shape[2] // HD
    positions = (lengths[None, :] + jnp.arange(step_count, dtype=jnp.int32)[:, None]).reshape(
        row_count
    )
    query = rotate_pairs(projected[0].reshape(row_count, heads_local, HD), positions).astype(
        jnp.bfloat16
    )
    new_keys = rotate_pairs(projected[1].reshape(row_count, heads_local, HD), positions).astype(
        jnp.bfloat16
    )
    new_values = projected[2].reshape(row_count, heads_local, HD).astype(jnp.bfloat16)
    query = query.reshape(step_count, request_count, heads_local, HD)
    new_keys = new_keys.reshape(step_count, request_count, heads_local, HD)
    new_values = new_values.reshape(step_count, request_count, heads_local, HD)
    score_scale = 1.0 / HD**0.5
    block_len = cache_keys.shape[1]
    key_block = cache_keys.reshape(request_count, block_len, heads_local, HD)
    value_block = cache_values.reshape(request_count, block_len, heads_local, HD)
    first_pos = lax.axis_index("seq") * block_len
    scores = (
        jnp.einsum("trhd,rchd->rthc", query, key_block, preferred_element_type=jnp.float32)
        * score_scale
    )
    places = first_pos + jnp.arange(block_len, dtype=jnp.int32)
    valid = (places[None, :] < lengths[:, None])[:, None, None, :]
    block_top = jnp.max(jnp.where(valid, scores, NEG_FILL), axis=-1)
    weights = jnp.where(valid, jnp.exp(scores - block_top[..., None]), 0.0)
    block_total = jnp.sum(weights, axis=-1)
    block_acc = jnp.einsum(
        "rthc,rchd->rthd",
        weights.astype(jnp.bfloat16),
        value_block,
        preferred_element_type=jnp.float32,
    )
    cache_top = lax.pmax(block_top, "seq")
    rescale = jnp.exp(block_top - cache_top)
    cache_total, cache_acc = lax.psum(
        (rescale * block_total, rescale[..., None] * block_acc), "seq"
    )
    new_scores = (
        jnp.einsum("trhd,urhd->rthu", query, new_keys, preferred_element_type=jnp.float32)
        * score_scale
    )
    causal = (jnp.arange(step_count)[:, None] >= jnp.arange(step_count)[None, :])[None, :, None, :]
    new_top = jnp.max(jnp.where(causal, new_scores, NEG_FILL), axis=-1)
    new_weights = jnp.where(causal, jnp.exp(new_scores - new_top[..., None]), 0.0)
    new_total = jnp.sum(new_weights, axis=-1)
    new_acc = jnp.einsum(
        "rthu,urhd->rthd",
        new_weights.astype(jnp.bfloat16),
        new_values,
        preferred_element_type=jnp.float32,
    )
    overall, denom, numer = combine_parts(
        (cache_top, cache_total, cache_acc), (new_top, new_total, new_acc)
    )
    attended = (
        (numer / denom[..., None])
        .transpose(1, 0, 2, 3)
        .reshape(row_count, heads_local * HD)
        .astype(jnp.bfloat16)
    )
    branch = lax.psum(
        jnp.dot(attended, attn_out_weight, preferred_element_type=jnp.float32), "head"
    )
    resid = inputs + branch
    normed_two = norm_rows(resid).astype(jnp.bfloat16)
    both = lax.psum(
        jnp.einsum("nd,kdf->knf", normed_two, ffn_in_weight, preferred_element_type=jnp.float32),
        "seq",
    )
    hidden = (jax.nn.silu(both[0]) * both[1]).astype(jnp.bfloat16)
    mlp_out = lax.psum(jnp.dot(hidden, ffn_out_weight, preferred_element_type=jnp.float32), "head")
    attn_branch = branch.astype(jnp.bfloat16).reshape(step_count, request_count, width_local)
    mlp_branch = mlp_out.astype(jnp.bfloat16).reshape(step_count, request_count, width_local)
    return (attn_branch, mlp_branch)


def solution(mesh):
    in_specs = (
        P(None, None, "seq"),
        P(None, "seq", "head"),
        P("head", "seq"),
        P(None, "seq", "head"),
        P("head", "seq"),
        P(None, "seq", "head"),
        P(None, "seq", "head"),
        P(),
    )
    out_specs = (P(None, None, "seq"), P(None, None, "seq"))
    return jax.shard_map(
        per_device, mesh=mesh, in_specs=in_specs, out_specs=out_specs, check_vma=False
    )
```

profile of v0, /device:TPU:1, one launch (start us, length us, event | category | flops | bytes accessed | tf_op | source)
XLA Modules:
  0.0 1064.0 jit_solution(13538129138450681759)
XLA Ops:
  7.2 0.0 copy-start
  7.2 0.0 all-reduce.4.cloned.1.call-start
  7.2 0.8 convert_reduce_fusion
  8.1 0.1 reduce_sum.59
  8.1 64.6 %psum.70 = f32[64]{0:T(128)S(1)} all-reduce(f32[64]{0:T(128)S(1)} %reduce_sum.59), channel_id=1, replica_groups=mesh['head'=8,'seq'=32] {'seq'}, use_global_device_ids=true, to_apply=%region_1.0 | all-reduce | flops 64 | bytes 512 | tf_op jit(solution)/shard_map/psum | solution.py:15
  72.7 0.1 sub.56
  72.8 0.9 fusion.41
  73.7 0.1 reduce_sum.61
  73.8 56.1 %psum.71 = f32[64]{0:T(128)S(1)} all-reduce(f32[64]{0:T(128)S(1)} %reduce_sum.61), channel_id=1, replica_groups=mesh['head'=8,'seq'=32] {'seq'}, use_global_device_ids=true, to_apply=%region_3.0 | all-reduce | flops 64 | bytes 512 | tf_op jit(solution)/shard_map/psum | solution.py:17
  129.9 0.8 fusion.43
  130.7 1.7 convolution_bitcast_fusion.1
  132.4 0.0 all-reduce.4.cloned.1.call-update
  132.4 0.0 all-reduce.6.cloned.1.call-start
  132.5 0.7 add_convert_fusion.2
  133.2 0.1 convert_element_type.65
  133.3 0.2 multiply_cosine_fusion
  133.5 0.7 broadcast_compare_fusion
  134.2 160.3 %all-reduce.4.cloned.1.call-done = f32[3,64,256]{2,1,0:T(8,128)} async-done(((f32[3,64,256]{2,1,0:T(8,128)}), f32[3,64,256]{2,1,0:T(8,128)}) %all-reduce.4.cloned.1.call-update) | async-done | bytes 196624 | tf_op jit(solution)/shard_map/psum | solution.py:65
  294.5 0.9 fusion.64
  295.5 0.2 fusion.65
  295.8 0.2 fusion.36
  296.1 0.1 copy.70
  296.2 0.1 fusion.49
  296.3 0.1 fusion.56
  296.4 0.1 copy.71
  296.5 0.1 copy.76
  296.6 3.5 select_reduce_fusion
  300.1 112.6 %pmax.7 = f32[16,4,2]{1,2,0:T(2,128)S(1)} all-reduce(f32[16,4,2]{1,2,0:T(2,128)S(1)} %get-tuple-element.26), channel_id=1, replica_groups=mesh['head'=8,'seq'=32] {'seq'}, use_global_device_ids=true, to_apply=%region_6.7 | all-reduce | flops 128 | bytes 1024 | tf_op jit(solution)/shard_map/pmax | solution.py:100
  412.7 0.3 fusion.25
  413.0 110.6 %psum.74 = f32[16,4,2]{1,2,0:T(2,128)S(1)} all-reduce(f32[16,4,2]{1,2,0:T(2,128)S(1)} %bitcast.130), channel_id=1, replica_groups=mesh['head'=8,'seq'=32] {'seq'}, use_global_device_ids=true, to_apply=%region_10.11 | all-reduce | flops 128 | bytes 1024 | tf_op jit(solution)/shard_map/psum | solution.py:102
  523.6 3.6 fusion.18
  527.2 0.0 all-reduce.6.cloned.1.call-update
  527.2 0.0 all-reduce.8.cloned.1.call-start
  527.3 0.8 slice.57
  528.1 0.1 copy.75
  528.3 190.0 %all-reduce.6.cloned.1.call-done = f32[16,4,2,128]{3,1,2,0:T(4,128)} async-done(((f32[16,4,2,128]{3,1,2,0:T(4,128)}), f32[16,4,2,128]{3,1,2,0:T(4,128)}) %all-reduce.6.cloned.1.call-update) | async-done | bytes 65552 | tf_op jit(solution)/shard_map/psum | solution.py:102
  718.3 1.0 fusion.22
  719.4 0.1 fusion.33
  719.5 24.8 %psum.75 = f32[64,64]{1,0:T(8,128)S(1)} all-reduce(f32[64,64]{1,0:T(8,128)S(1)} %fusion.33), channel_id=1, replica_groups=mesh['head'=8,'seq'=32] {'head'}, use_global_device_ids=true, to_apply=%region_12.13 | all-reduce | flops 4096 | bytes 32768 | tf_op jit(solution)/shard_map/psum | solution.py:128
  744.2 0.1 fusion.55
  744.3 59.2 %psum.76 = f32[64]{0:T(128)S(1)} all-reduce(f32[64]{0:T(128)S(1)} %fusion.55), channel_id=1, replica_groups=mesh['head'=8,'seq'=32] {'seq'}, use_global_device_ids=true, to_apply=%region_14.15 | all-reduce | flops 64 | bytes 512 | tf_op jit(solution)/shard_map/psum | solution.py:15
  803.5 0.7 multiply_reduce_fusion
  804.3 55.9 %psum.77 = f32[64]{0:T(128)S(1)} all-reduce(f32[64]{0:T(128)S(1)} %get-tuple-element.19), channel_id=1, replica_groups=mesh['head'=8,'seq'=32] {'seq'}, use_global_device_ids=true, to_apply=%region_16.17 | all-reduce | flops 64 | bytes 512 | tf_op jit(solution)/shard_map/psum | solution.py:17
  860.2 1.1 convolution_bitcast_fusion
  861.3 0.0 all-reduce.8.cloned.1.call-update
  861.3 169.1 %all-reduce.8.cloned.1.call-done = f32[2,64,1024]{2,1,0:T(8,128)} async-done(((f32[2,64,1024]{2,1,0:T(8,128)}), f32[2,64,1024]{2,1,0:T(8,128)}) %all-reduce.8.cloned.1.call-update) | async-done | bytes 524304 | tf_op jit(solution)/shard_map/psum | solution.py:133
  1030.4 1.2 fusion.31
  1031.6 25.9 %psum.79 = bf16[64,64]{1,0:T(8,128)(2,1)} all-reduce(f32[64,64]{1,0:T(8,128)S(1)} %fusion.31), channel_id=1, replica_groups=mesh['head'=8,'seq'=32] {'head'}, use_global_device_ids=true, to_apply=%region_18.19 | all-reduce | flops 4096 | bytes 24576 | tf_op jit(solution)/shard_map/psum | solution.py:138
  (25 shorter events, 0.3 us)
Async XLA Ops:
  7.2 853.0 %copy-start = (bf16[2,64,1024]{2,1,0:T(8,128)(2,1)S(1)}, bf16[2,64,1024]{2,1,0:T(8,128)(2,1)}, u32[]{:S(2)}) copy-start(bf16[2,64,1024]{2,1,0:T(8,128)(2,1)} %param.11) | copy-start | bytes 786436
  7.2 287.3 %all-reduce.4.cloned.1.call-start = ((), (), s32[]{:S(2)}) async-start(), calls=%async_computation | async-start | bytes 393216 | tf_op jit(solution)/shard_map/psum | solution.py:65
  132.4 585.9 %all-reduce.6.cloned.1.call-start = ((), (), s32[]{:S(2)}) async-start(), calls=%async_computation.1 | async-start | bytes 131072 | tf_op jit(solution)/shard_map/psum | solution.py:102
  523.6 195.8 %copy-start.2 = (bf16[256,64]{0,1:T(8,128)(2,1)S(1)}, bf16[256,64]{0,1:T(8,128)(2,1)}, u32[]{:S(2)}) copy-start(bf16[256,64]{0,1:T(8,128)(2,1)} %param.10) | copy-start | bytes 98308
  523.6 220.6 %copy-start.1 = (bf16[4,16,64]{2,1,0:T(8,128)(2,1)S(1)}, bf16[4,16,64]{2,1,0:T(8,128)(2,1)}, u32[]{:S(2)}) copy-start(bf16[4,16,64]{2,1,0:T(8,128)(2,1)} %param.8) | copy-start | bytes 24580
  523.6 506.8 %copy-start.3 = (bf16[1024,64]{0,1:T(8,128)(2,1)S(1)}, bf16[1024,64]{0,1:T(8,128)(2,1)}, u32[]{:S(2)}) copy-start(bf16[1024,64]{0,1:T(8,128)(2,1)} %param.12) | copy-start | bytes 393220
  527.2 503.2 %all-reduce.8.cloned.1.call-start = ((), (), s32[]{:S(2)}) async-start(), calls=%async_computation.2 | async-start | bytes 1048576 | tf_op jit(solution)/shard_map/psum | solution.py:133
Sparse Core Ops, SparseCore 0:
  132.5 161.9 all-reduce.3
  527.3 190.9 all-reduce.5
  861.4 168.9 all-reduce.7
where the time goes:
time: 1070 us; the launch traced here: 1060 us
  waiting for transfers between devices  519 us (49%)
  blocking collectives  510 us (48%)
  between operations  13.9 us (1%)
  matrix products  12.5 us (1%)
    psum x1, waiting for transfers between devices, per_device(): lax.psum((rescale * block_total, rescale[..., None] * block_acc), 'seq')  190 us
    psum x1, waiting for transfers between devices, per_device(): lax.psum(jnp.einsum('nd,kdf->knf', normed_two, ffn_in_weight, preferred_e...  169 us
    psum x1, waiting for transfers between devices, per_device(): projected = lax.psum(partial_qkv, 'seq')  160 us
    psum x2, blocking collectives, norm_rows(): center = lax.psum(jnp.sum(values, axis=-1), 'seq') / D  124 us
    pmax x1, blocking collectives, per_device(): cache_top = lax.pmax(block_top, 'seq')  113 us
    psum x2, blocking collectives, norm_rows(): spread = lax.psum(jnp.sum(deviate * deviate, axis=-1), 'seq') / D  112 us
    psum x1, blocking collectives, per_device(): lax.psum((rescale * block_total, rescale[..., None] * block_acc), 'seq')  111 us
    psum x1, blocking collectives, per_device(): lax.psum(jnp.dot(hidden, ffn_out_weight, preferred_element_type=jnp.float...  25.9 us
  transfers between devices with their start and end apart: 3, of which 3 were waited for; matrix products, arithmetic and copies ran while one was open for 0% of the time, Pallas kernels for 0%

commit v1 on v0

v1 whole, which is shorter than its diff:
```python
import functools

import numpy as np
import jax
import jax.numpy as jnp
from jax import lax
from jax.experimental import pallas as pl
from jax.experimental.pallas import tpu as pltpu
from jax.sharding import PartitionSpec as P

D = 2048
HD = 128
EPS = 1e-05
NEG = -1e30
SCALE = 1.0 / HD**0.5
F32 = jnp.float32
BF = jnp.bfloat16
NT = (((1,), (1,)), ((), ()))
TN = (((0,), (0,)), ((), ()))
VM = pl.BlockSpec(memory_space=pltpu.VMEM)
PARAMS = pltpu.CompilerParams(vmem_limit_bytes=16 << 20)


def iota(shape, axis):
    return lax.broadcasted_iota(jnp.int32, shape, axis)


def mm(a, b, dims=(((1,), (0,)), ((), ()))):
    return lax.dot_general(a, b, dims, preferred_element_type=F32)


def one_hot(cond):
    return jnp.where(cond, 1.0, 0.0).astype(BF)


def to_request_major():
    n, m = iota((64, 64), 0), iota((64, 64), 1)
    return one_hot(m == (n & 3) * 16 + (n >> 2))


def to_step_major():
    m, n = iota((64, 64), 0), iota((64, 64), 1)
    return one_hot(n == (m & 15) * 4 + (m >> 4))


def split(v):
    hi = v.astype(BF).astype(F32)
    return jnp.concatenate([hi, v - hi], axis=1)


def qkv_kernel(x_ref, w_ref, out_ref):
    xp = mm(to_request_major(), x_ref[...])
    center = jnp.mean(xp, axis=1, keepdims=True)
    dev = xp - center
    spread = jnp.sum(dev * dev, axis=1, keepdims=True)
    rows = jnp.concatenate([xp, jnp.ones((16, 64), F32)], axis=0).astype(BF)
    lane, row = iota((64, 128), 1), iota((64, 128), 0)
    placed = jnp.where(lane == (row & 3), center, 0.0) + jnp.where(lane == 4 + (row & 3), spread, 0.0)
    pick = jnp.where(iota((16, 64), 0) == (iota((16, 64), 1) >> 2), 1.0, 0.0)
    stats = lax.dot_general(
        pick, placed, (((1,), (0,)), ((), ())), precision=lax.Precision.HIGHEST, preferred_element_type=F32
    )
    for k in range(3):
        part = mm(rows, w_ref[k])
        for p in range(2):
            cols = part[:, p * 128 : (p + 1) * 128]
            for r in range(16):
                out_ref[2 * r + p, :, k * 128 : (k + 1) * 128] = cols[4 * r : 4 * r + 4]
                out_ref[2 * r + p, k : k + 1, 384:512] = cols[64:65]
    for r in range(16):
        for p in range(2):
            out_ref[2 * r + p, 3:4, 384:512] = stats[r : r + 1]


def rope_kernel(got_ref, cos_ref, sin_ref, q_ref, new_ref):
    total = jnp.sum(got_ref[...], axis=0)
    stats = jnp.concatenate([got_ref[i, 3:4, 384:512] for i in range(32)], axis=0)
    center = jnp.sum(stats, axis=0, keepdims=True) * (1.0 / 32)
    dev = stats - center
    between = jnp.sum(dev * dev, axis=0, keepdims=True) * 64.0
    within = jnp.sum(stats, axis=0, keepdims=True)
    lane, row = iota((4, 128), 1), iota((4, 128), 0)
    mean = jnp.sum(jnp.where(lane == row, center, 0.0), axis=1, keepdims=True)
    var = jnp.sum(
        jnp.where(lane == row, between, 0.0) + jnp.where(lane == row + 4, within, 0.0), axis=1, keepdims=True
    ) * (1.0 / D)
    rstd = lax.rsqrt(var + EPS)
    q, k, v = (
        rstd * (total[:, j * 128 : (j + 1) * 128] - mean * total[j : j + 1, 384:512]) for j in range(3)
    )
    cos, sin = cos_ref[...], sin_ref[...]
    q = (q * cos + pltpu.roll(q, 64, 1) * sin).astype(BF).astype(F32)
    k = (k * cos + pltpu.roll(k, 64, 1) * sin).astype(BF).astype(F32)
    v = v.astype(BF).astype(F32)
    place = lax.axis_index("seq")
    both = jnp.concatenate([q, q], axis=0)
    mine = (iota((8, 128), 0) >> 2) == (place & 1)
    q_ref[...] = jnp.broadcast_to(jnp.where(mine, both, 0.0).astype(BF)[None], (32, 8, 128))
    step = iota((4, 1), 0)
    scores = [
        jnp.where(step >= u, jnp.sum(q * k[u : u + 1], axis=1, keepdims=True) * SCALE, NEG) for u in range(4)
    ]
    top = jnp.maximum(jnp.maximum(scores[0], scores[1]), jnp.maximum(scores[2], scores[3]))
    weights = [jnp.where(step >= u, jnp.exp(scores[u] - top), 0.0) for u in range(4)]
    acc = sum(weights[u].astype(BF).astype(F32) * v[u : u + 1] for u in range(4))
    mass = weights[0] + weights[1] + weights[2] + weights[3]
    new_ref[0:4, :] = acc
    new_ref[4:8, :] = jnp.where(lane < 64, top, mass)


def attend_kernel(len_ref, q_ref, k_ref, v_ref, out_ref):
    group = pl.program_id(0)
    first = lax.axis_index("seq") * 512
    places = first + iota((8, 512), 1)
    row, lane = iota((8, 128), 0), iota((8, 128), 1)
    for j in range(4):
        valid = places < len_ref[group * 4 + j]
        q = jnp.concatenate([q_ref[2 * j], q_ref[2 * j + 1]], axis=1)
        scores = jnp.where(valid, mm(q, k_ref[j], NT) * SCALE, NEG)
        top = jnp.max(scores, axis=1, keepdims=True)
        weights = jnp.where(valid, jnp.exp(scores - top), 0.0)
        mass = jnp.sum(weights, axis=1, keepdims=True)
        acc = mm(weights.astype(BF), v_ref[j])
        stats = jnp.where(lane < 64, top, mass)
        out_ref[2 * j] = jnp.where(row < 4, acc[:, :128], pltpu.roll(stats, 4, 0))
        out_ref[2 * j + 1] = jnp.where(row < 4, pltpu.roll(acc[:, 128:], 4, 0), stats)


def combine_kernel(got_ref, new_ref, out_ref):
    row, lane = iota((8, 128), 0), iota((8, 128), 1)

    def parts(block):
        stats = pltpu.roll(block, 4, 0)
        other = pltpu.roll(stats, 64, 1)
        return jnp.where(lane < 64, stats, other), jnp.where(lane < 64, other, stats), block

    blocks = [parts(got_ref[i]) for i in range(32)] + [parts(new_ref[...])]
    top = functools.reduce(jnp.maximum, [b[0] for b in blocks])
    numer = jnp.zeros((8, 128), F32)
    denom = jnp.zeros((8, 128), F32)
    for block_top, mass, acc in blocks:
        factor = jnp.exp(block_top - top)
        numer = numer + factor * acc
        denom = denom + factor * mass
    attended = jnp.where(row < 4, numer / jnp.where(row < 4, denom, 1.0), 0.0)
    odd = (lax.axis_index("seq") >> 1) & 1
    placed = jnp.where(odd == 1, pltpu.roll(attended, 4, 0), attended)
    out_ref[...] = jnp.broadcast_to(placed.astype(BF)[None], (32, 8, 128))


def pack(v):
    return jnp.concatenate([v[0:32], v[32:64]], axis=1)


def unpack(v):
    return jnp.concatenate([v[:, 0:64], v[:, 64:128]], axis=0)


def out_proj_kernel(got_ref, w_ref, out_ref):
    got = got_ref[...].astype(F32).reshape(8, 2, 2, 8, 128)
    rows = got[:, 0] + got[:, 1]
    attended = jnp.concatenate([rows[:, 0].reshape(64, 128), rows[:, 1].reshape(64, 128)], axis=1).astype(BF)
    part = mm(w_ref[...], attended, NT)
    out_ref[...] = jnp.broadcast_to(pack(part)[None], (8, 32, 128))


def ffn_in_kernel(got_ref, x_ref, w_ref, branch_ref, out_ref):
    branch = unpack(jnp.sum(got_ref[...], axis=0))
    branch_ref[...] = mm(to_step_major(), branch.astype(BF), NT).astype(BF)
    eye = one_hot(iota((64, 64), 0) == iota((64, 64), 1))
    xt = mm(eye, mm(to_request_major(), x_ref[...]).astype(BF), NT)
    resid = xt + branch
    center = jnp.mean(resid, axis=0, keepdims=True)
    dev = resid - center
    spread = jnp.sum(dev * dev, axis=0, keepdims=True)
    zero = jnp.zeros((64, 64), F32)
    both = jnp.concatenate(
        [jnp.concatenate([dev, zero], axis=1), jnp.concatenate([zero, dev], axis=1)], axis=0
    ).astype(BF)
    weight = w_ref[...].reshape(128, 1024)
    prod = mm(weight, both, TN).astype(BF)
    out_ref[:, 0:16, :] = prod[0:512].reshape(32, 16, 128)
    out_ref[:, 16:32, :] = prod[512:1024].reshape(32, 16, 128)
    ones = jnp.ones((8, 64), BF)
    unit, slot = iota((32, 512), 1), iota((32, 512), 0)
    sums = jnp.zeros((32, 128), F32)
    for kind in range(2):
        cols = mm(ones, w_ref[kind])[0:1]
        for half in range(2):
            chosen = jnp.where((unit >> 4) == slot, cols[:, half * 512 : half * 512 + 512], 0.0).astype(BF)
            spot = one_hot(iota((512, 128), 1) == kind * 64 + half * 16 + (iota((512, 128), 0) & 15))
            sums = sums + mm(chosen, spot)
    row = iota((8, 128), 0)
    head = jnp.where(row == 0, split(center), jnp.where(row == 1, split(spread), 0.0))
    for s in range(32):
        out_ref[s, 32:40, :] = jnp.where(row == 2, sums[s : s + 1], head).astype(BF)


def hidden_kernel(got_ref, out_ref):
    total = jnp.sum(got_ref[:, 0:32, :].astype(F32), axis=0)
    extra = [got_ref[i, 32:40, :].astype(F32) for i in range(32)]
    center = jnp.concatenate([e[0:1] for e in extra], axis=0)
    center = center[:, 0:64] + center[:, 64:128]
    within = jnp.sum(jnp.concatenate([e[1:2] for e in extra], axis=0), axis=0, keepdims=True)
    within = within[:, 0:64] + within[:, 64:128]
    sums = jnp.concatenate([e[2:3] for e in extra], axis=0)
    mean = jnp.sum(center, axis=0, keepdims=True) * (1.0 / 32)
    shift = center - mean
    var = (within + 64.0 * jnp.sum(shift * shift, axis=0, keepdims=True)) * (1.0 / D)
    rstd = lax.rsqrt(var + EPS)
    fix = mm(sums.astype(BF), shift.astype(BF), TN)
    gate = rstd * (total[:, 0:64] + fix[0:32])
    up = rstd * (total[:, 64:128] + fix[64:96])
    hidden = gate / (1.0 + jnp.exp(-gate)) * up
    packed = jnp.concatenate([hidden[0:16], hidden[16:32]], axis=1).astype(BF)
    out_ref[...] = jnp.broadcast_to(packed[None], (32, 16, 128))


def ffn_out_kernel(got_ref, w_ref, out_ref):
    hidden = got_ref[...].reshape(512, 128)
    low = mm(w_ref[:, 0:512], hidden)
    high = mm(w_ref[:, 512:1024], hidden)
    part = low[:, 0:64] + high[:, 64:128]
    out_ref[...] = jnp.broadcast_to(pack(part)[None], (8, 32, 128))


def final_kernel(got_ref, out_ref):
    total = unpack(jnp.sum(got_ref[...], axis=0))
    out_ref[...] = mm(to_step_major(), total.astype(BF), NT).astype(BF)


def call(kernel, n_in, *outs):
    shapes = [jax.ShapeDtypeStruct(shape, dtype) for shape, dtype in outs]
    one = len(shapes) == 1
    return pl.pallas_call(
        kernel,
        out_shape=shapes[0] if one else shapes,
        in_specs=[VM] * n_in,
        out_specs=VM if one else [VM] * len(shapes),
        compiler_params=PARAMS,
    )


def exchange(values, axis):
    return lax.all_to_all(values, axis, 0, 0, tiled=False)


def per_device(
    tokens, attn_in_weight, attn_out_weight, ffn_in_weight, ffn_out_weight, cache_keys, cache_values, lengths
):
    x = tokens.reshape(64, 64)
    place = lax.axis_index("seq")
    freq = (10000.0 ** (-2.0 * np.arange(64) / HD)).astype(np.float32)
    freq = jnp.asarray(np.concatenate([freq, freq]))
    length = lax.dynamic_slice(lengths, (place // 2,), (1,))
    angles = (length + jnp.arange(4, dtype=jnp.int32)).astype(F32)[:, None] * freq[None, :]
    sign = jnp.asarray(np.concatenate([-np.ones(64, np.float32), np.ones(64, np.float32)]))
    cos, sin = jnp.cos(angles), jnp.sin(angles) * sign[None, :]

    got = exchange(call(qkv_kernel, 2, ((32, 4, 512), F32))(x, attn_in_weight), "seq")
    queries, new = call(rope_kernel, 3, ((32, 8, 128), BF), ((8, 128), F32))(got, cos, sin)
    queries = exchange(queries, "seq")
    blocks = pl.pallas_call(
        attend_kernel,
        out_shape=jax.ShapeDtypeStruct((32, 8, 128), F32),
        grid=(4,),
        in_specs=[
            pl.BlockSpec(memory_space=pltpu.SMEM),
            pl.BlockSpec((8, 8, 128), lambda g: (g, 0, 0)),
            pl.BlockSpec((4, 512, 256), lambda g: (g, 0, 0)),
            pl.BlockSpec((4, 512, 256), lambda g: (g, 0, 0)),
        ],
        out_specs=pl.BlockSpec((8, 8, 128), lambda g: (g, 0, 0)),
        compiler_params=pltpu.CompilerParams(vmem_limit_bytes=24 << 20),
    )(lengths, queries, cache_keys, cache_values)
    attended = exchange(call(combine_kernel, 2, ((32, 8, 128), BF))(exchange(blocks, "seq"), new), "seq")
    part = call(out_proj_kernel, 2, ((8, 32, 128), F32))(attended, attn_out_weight.T)
    branch, part = call(ffn_in_kernel, 3, ((64, 64), BF), ((32, 40, 128), BF))(
        exchange(part, "head"), x, ffn_in_weight
    )
    hidden = exchange(call(hidden_kernel, 1, ((32, 16, 128), BF))(exchange(part, "seq")), "seq")
    part = call(ffn_out_kernel, 2, ((8, 32, 128), F32))(hidden, ffn_out_weight.T)
    mlp = call(final_kernel, 1, ((64, 64), BF))(exchange(part, "head"))
    return branch.reshape(4, 16, 64), mlp.reshape(4, 16, 64)


def solution(mesh):
    in_specs = (
        P(None, None, "seq"),
        P(None, "seq", "head"),
        P("head", "seq"),
        P(None, "seq", "head"),
        P("head", "seq"),
        P(None, "seq", "head"),
        P(None, "seq", "head"),
        P(),
    )
    out_specs = (P(None, None, "seq"), P(None, None, "seq"))
    return jax.shard_map(per_device, mesh=mesh, in_specs=in_specs, out_specs=out_specs, check_vma=False)
```

time: 1070 us -> 134 us (0.13)
  waiting for transfers between devices: 519 us -> 8.49 us
  blocking collectives: 510 us -> 92.6 us
  between operations: 13.9 us -> 0.72 us
  matrix products: 12.5 us -> 0 us
  starting transfers between devices: 0.12 us -> 12 us
    psum x3 -> x0, waiting for transfers between devices: 519 us -> none  [the longest x1 190 us: per_device(): lax.psum((rescale * block_total, rescale[..., None] * block_acc), 'seq')]
    psum x7 -> x0, blocking collectives: 397 us -> none  [the longest x2 124 us: norm_rows(): center = lax.psum(jnp.sum(values, axis=-1), 'seq') / D]
    pmax x1 -> x0, blocking collectives: 113 us -> none  [per_device(): cache_top = lax.pmax(block_top, 'seq')]
    all_to_all x0 -> x7, blocking collectives: none -> 92.6 us  [exchange(): return lax.all_to_all(values, axis, 0, 0, tiled=False)]
    dot_general x8 -> x0, matrix products: 12.5 us -> none  [the longest x1 3.57 us: per_device(): jnp.einsum('rthc,rchd->rthd', weights.astype(jnp.bfloat16), value_block,...]
    all_to_all x0 -> x1, starting transfers between devices: none -> 12 us  [exchange(): return lax.all_to_all(values, axis, 0, 0, tiled=False)]
  transfers between devices with their start and end apart: 3 -> 1, of which waited for: 3 -> 1; matrix products, arithmetic and copies ran while one was open for 0% -> 2% of each run, Pallas kernels for 0% -> 0%
where the time goes in v1:
time: 134 us; the launch traced here: 133 us
  blocking collectives  92.6 us (69%)
  starting transfers between devices  12 us (9%)
  Pallas kernels  10.3 us (8%)
  waiting for transfers between devices  8.49 us (6%)
  local copies, waits for them, and re-layouts  7.89 us (6%)
  other arithmetic  1.43 us (1%)
    all_to_all x7, blocking collectives, exchange(): return lax.all_to_all(values, axis, 0, 0, tiled=False)  92.6 us
    all_to_all x1, starting transfers between devices, exchange(): return lax.all_to_all(values, axis, 0, 0, tiled=False)  12 us
    all_to_all x1, waiting for transfers between devices, exchange(): return lax.all_to_all(values, axis, 0, 0, tiled=False)  8.49 us
    unnamed x18, local copies, waits for them, and re-layouts  6.65 us
    pallas_call x1, Pallas kernels, per_device(): pl.pallas_call(attend_kernel, out_shape=jax.ShapeDtypeStruct((32, 8, 128)...  5.93 us
  transfers between devices with their start and end apart: 1, of which 1 were waited for; matrix products, arithmetic and copies ran while one was open for 2% of the time, Pallas kernels for 0%

profile of v1, /device:TPU:1, one launch (start us, length us, event | category | flops | bytes accessed | tf_op | source)
XLA Modules:
  0.0 133.5 jit_solution(848464390404587490)
XLA Ops:
  0.6 0.0 copy-start.4
  0.6 0.9 copy-done.4
  1.5 0.0 copy-start.5
  1.5 0.7 copy-done.5
  2.2 1.2 shard_map.113
  3.4 12.0 %all-to-all-start = ((f32[32,4,512]{2,1,0:T(4,128)}), f32[32,4,512]{2,1,0:T(4,128)S(1)}, u32[]{:S(2)}, u32[]{:S(2)}) async-start(f32[32,4,512]{2,1,0:T(4,128)} %shard_map.113), calls=%async_computation | async-start | bytes 524288 | tf_op jit(solution)/shard_map/all_to_all | solution.py:245
  15.5 1.2 dynamic_slice.3
  16.7 0.6 add_convert_fusion
  17.4 0.8 fusion
  18.2 8.5 %all-to-all-done.got_ref = f32[32,4,512]{2,1,0:T(4,128)S(1)} async-done(((f32[32,4,512]{2,1,0:T(4,128)}), f32[32,4,512]{2,1,0:T(4,128)S(1)}, u32[]{:S(2)}, u32[]{:S(2)}) %all-to-all-start) | async-done | bytes 262176 | tf_op jit(solution)/shard_map/all_to_all | solution.py:245
  26.6 0.3 shard_map.114
  26.9 13.4 %all_to_all.40.q_ref = bf16[32,8,128]{2,1,0:T(8,128)(2,1)S(1)} all-to-all(bf16[32,8,128]{2,1,0:T(8,128)(2,1)S(1)} %get-tuple-element.6), channel_id=1, replica_groups=mesh['head'=8,'seq'=32] {'seq'}, dimensions={0} | all-to-all | bytes 131072 | tf_op jit(solution)/shard_map/all_to_all | solution.py:245
  40.3 0.0 copy-start
  40.3 2.2 %copy-done = bf16[16,512,256]{2,1,0:T(8,128)(2,1)S(1)} copy-done((bf16[16,512,256]{2,1,0:T(8,128)(2,1)S(1)}, bf16[16,512,256]{2,1,0:T(8,128)(2,1)}, u32[]{:S(2)}) %copy-start) | copy-done | bytes 4194328
  42.5 0.0 copy-start.1
  42.5 2.2 %copy-done.1 = bf16[16,512,256]{2,1,0:T(8,128)(2,1)S(1)} copy-done((bf16[16,512,256]{2,1,0:T(8,128)(2,1)S(1)}, bf16[16,512,256]{2,1,0:T(8,128)(2,1)}, u32[]{:S(2)}) %copy-start.1) | copy-done | bytes 4194328
  44.7 0.0 copy-start.8
  44.7 0.7 copy-done.8
  45.3 0.0 copy-start.7
  45.4 0.0 copy-start.2
  45.4 0.0 copy-start.6
  45.4 0.0 copy-start.3
  45.4 5.9 %shard_map.115 = f32[32,8,128]{2,1,0:T(8,128)S(1)} custom-call(s32[16]{0:T(128)S(1)} %copy-done.8, bf16[32,8,128]{2,1,0:T(8,128)(2,1)S(1)} %all_to_all.40.q_ref, bf16[16,512,256]{2,1,0:T(8,128)(2,1)S(1)} %copy-done, bf16[16,512,256]{2,1,0:T(8,128)(2,1)S(1)} %copy-done.1), custom_call_target="tpu_custom_call" | custom-call | tf_op jit(solution)/shard_map/pallas_call | solution.py:263
  51.3 12.5 %all_to_all.41.got_ref = f32[32,8,128]{2,1,0:T(8,128)S(1)} all-to-all(f32[32,8,128]{2,1,0:T(8,128)S(1)} %shard_map.115), channel_id=1, replica_groups=mesh['head'=8,'seq'=32] {'seq'}, dimensions={0} | all-to-all | bytes 262144 | tf_op jit(solution)/shard_map/all_to_all | solution.py:245
  63.8 0.2 shard_map.116
  63.9 12.0 %all_to_all.42.got_ref = bf16[32,8,128]{2,1,0:T(8,128)(2,1)S(1)} all-to-all(bf16[32,8,128]{2,1,0:T(8,128)(2,1)S(1)} %shard_map.116), channel_id=1, replica_groups=mesh['head'=8,'seq'=32] {'seq'}, dimensions={0} | all-to-all | bytes 131072 | tf_op jit(solution)/shard_map/all_to_all | solution.py:245
  75.9 0.0 copy-done.7
  76.0 0.2 shard_map.117
  76.2 14.6 %all_to_all.43.got_ref = f32[8,32,128]{2,1,0:T(8,128)S(1)} all-to-all(f32[8,32,128]{2,1,0:T(8,128)S(1)} %shard_map.117), channel_id=1, replica_groups=mesh['head'=8,'seq'=32] {'head'}, dimensions={0} | all-to-all | bytes 262144 | tf_op jit(solution)/shard_map/all_to_all | solution.py:245
  90.8 0.0 copy-done.2
  90.8 0.0 copy-done.6
  90.8 1.0 shard_map.118
  91.8 15.5 %all_to_all.44.got_ref = bf16[32,40,128]{2,1,0:T(8,128)(2,1)S(1)} all-to-all(bf16[32,40,128]{2,1,0:T(8,128)(2,1)S(1)} %get-tuple-element.9), channel_id=1, replica_groups=mesh['head'=8,'seq'=32] {'seq'}, dimensions={0} | all-to-all | bytes 655360 | tf_op jit(solution)/shard_map/all_to_all | solution.py:245
  107.3 0.4 shard_map.119
  107.7 13.8 %all_to_all.45.got_ref = bf16[32,16,128]{2,1,0:T(8,128)(2,1)S(1)} all-to-all(bf16[32,16,128]{2,1,0:T(8,128)(2,1)S(1)} %shard_map.119), channel_id=1, replica_groups=mesh['head'=8,'seq'=32] {'seq'}, dimensions={0} | all-to-all | bytes 262144 | tf_op jit(solution)/shard_map/all_to_all | solution.py:245
  121.5 0.0 copy-done.3
  121.5 0.3 shard_map.120
  121.9 10.8 %all_to_all.46.got_ref = f32[8,32,128]{2,1,0:T(8,128)S(1)} all-to-all(f32[8,32,128]{2,1,0:T(8,128)S(1)} %shard_map.120), channel_id=1, replica_groups=mesh['head'=8,'seq'=32] {'head'}, dimensions={0} | all-to-all | bytes 262144 | tf_op jit(solution)/shard_map/all_to_all | solution.py:245
  132.6 0.8 shard_map.121
Async XLA Ops:
  0.6 0.9 copy-start.4
  1.5 0.7 copy-start.5
  3.4 23.2 %all-to-all-start = ((f32[32,4,512]{2,1,0:T(4,128)}), f32[32,4,512]{2,1,0:T(4,128)S(1)}, u32[]{:S(2)}, u32[]{:S(2)}) async-start(f32[32,4,512]{2,1,0:T(4,128)} %shard_map.113), calls=%async_computation | async-start | bytes 524288 | tf_op jit(solution)/shard_map/all_to_all | solution.py:245
  40.3 2.2 %copy-start = (bf16[16,512,256]{2,1,0:T(8,128)(2,1)S(1)}, bf16[16,512,256]{2,1,0:T(8,128)(2,1)}, u32[]{:S(2)}) copy-start(bf16[16,512,256]{2,1,0:T(8,128)(2,1)} %k_ref.1) | copy-start | bytes 12582916
  42.5 2.2 %copy-start.1 = (bf16[16,512,256]{2,1,0:T(8,128)(2,1)S(1)}, bf16[16,512,256]{2,1,0:T(8,128)(2,1)}, u32[]{:S(2)}) copy-start(bf16[16,512,256]{2,1,0:T(8,128)(2,1)} %v_ref.1) | copy-start | bytes 12582916
  44.7 0.7 copy-start.8
  45.3 30.6 %copy-start.7 = (bf16[256,64]{0,1:T(8,128)(2,1)S(1)}, bf16[256,64]{0,1:T(8,128)(2,1)}, u32[]{:S(2)}) copy-start(bf16[256,64]{0,1:T(8,128)(2,1)} %param.12) | copy-start | bytes 98308
  45.4 45.4 %copy-start.2 = (bf16[2,64,1024]{2,1,0:T(8,128)(2,1)S(1)}, bf16[2,64,1024]{2,1,0:T(8,128)(2,1)}, u32[]{:S(2)}) copy-start(bf16[2,64,1024]{2,1,0:T(8,128)(2,1)} %w_ref.3) | copy-start | bytes 786436
  45.4 45.4 %copy-start.6 = (bf16[4,16,64]{2,1,0:T(8,128)(2,1)S(1)}, bf16[4,16,64]{2,1,0:T(8,128)(2,1)}, u32[]{:S(2)}) copy-start(bf16[4,16,64]{2,1,0:T(8,128)(2,1)} %param.10) | copy-start | bytes 24580
  45.4 76.2 %copy-start.3 = (bf16[1024,64]{0,1:T(8,128)(2,1)S(1)}, bf16[1024,64]{0,1:T(8,128)(2,1)}, u32[]{:S(2)}) copy-start(bf16[1024,64]{0,1:T(8,128)(2,1)} %param.14) | copy-start | bytes 393220

commit v2 on v1

--- a/solution.py
+++ b/solution.py
@@ -18,6 +18,7 @@
 NT = (((1,), (1,)), ((), ()))
 TN = (((0,), (0,)), ((), ()))
 VM = pl.BlockSpec(memory_space=pltpu.VMEM)
+LONG = pl.CostEstimate(flops=1 << 40, bytes_accessed=1 << 40, transcendentals=0)
 PARAMS = pltpu.CompilerParams(vmem_limit_bytes=16 << 20)
 
 
@@ -48,7 +49,27 @@
     return jnp.concatenate([hi, v - hi], axis=1)
 
 
-def qkv_kernel(x_ref, w_ref, out_ref):
+def rotation(position, coarse_ref, fine_ref):
+    lane = iota((4, 128), 1)
+    spots = [position + t for t in range(4)]
+    a = jnp.concatenate([coarse_ref[pl.ds(spot >> 7, 1), :] for spot in spots], axis=0)
+    b = jnp.concatenate([fine_ref[pl.ds(spot & 127, 1), :] for spot in spots], axis=0)
+    a_other, b_other = pltpu.roll(a, 64, 1), pltpu.roll(b, 64, 1)
+    first = lane < 64
+    side = a_other * jnp.where(first, b_other, b)
+    both = a * jnp.where(first, b, b_other) + jnp.where(first, -side, side)
+    other = pltpu.roll(both, 64, 1)
+    return jnp.where(first, both, other), jnp.where(first, -other, both)
+
+
+def qkv_kernel(x_hbm, w_hbm, out_ref, x_ref, w_ref, sems):
+    copies = [
+        pltpu.make_async_copy(x_hbm, x_ref, sems.at[0]),
+        pltpu.make_async_copy(w_hbm, w_ref, sems.at[1]),
+    ]
+    for copy in copies:
+        copy.start()
+    copies[0].wait()
     xp = mm(to_request_major(), x_ref[...])
     center = jnp.mean(xp, axis=1, keepdims=True)
     dev = xp - center
@@ -60,6 +81,7 @@
     stats = lax.dot_general(
         pick, placed, (((1,), (0,)), ((), ())), precision=lax.Precision.HIGHEST, preferred_element_type=F32
     )
+    copies[1].wait()
     for k in range(3):
         part = mm(rows, w_ref[k])
         for p in range(2):
@@ -72,7 +94,7 @@
             out_ref[2 * r + p, 3:4, 384:512] = stats[r : r + 1]
 
 
-def rope_kernel(got_ref, cos_ref, sin_ref, q_ref, new_ref):
+def rope_kernel(len_ref, got_ref, coarse_ref, fine_ref, q_ref, new_ref):
     total = jnp.sum(got_ref[...], axis=0)
     stats = jnp.concatenate([got_ref[i, 3:4, 384:512] for i in range(32)], axis=0)
     center = jnp.sum(stats, axis=0, keepdims=True) * (1.0 / 32)
@@ -88,7 +110,7 @@
     q, k, v = (
         rstd * (total[:, j * 128 : (j + 1) * 128] - mean * total[j : j + 1, 384:512]) for j in range(3)
     )
-    cos, sin = cos_ref[...], sin_ref[...]
+    cos, sin = rotation(len_ref[lax.axis_index("seq") >> 1], coarse_ref, fine_ref)
     q = (q * cos + pltpu.roll(q, 64, 1) * sin).astype(BF).astype(F32)
     k = (k * cos + pltpu.roll(k, 64, 1) * sin).astype(BF).astype(F32)
     v = v.astype(BF).astype(F32)
@@ -109,21 +131,21 @@
 
 
 def attend_kernel(len_ref, q_ref, k_ref, v_ref, out_ref):
-    group = pl.program_id(0)
     first = lax.axis_index("seq") * 512
     places = first + iota((8, 512), 1)
     row, lane = iota((8, 128), 0), iota((8, 128), 1)
-    for j in range(4):
-        valid = places < len_ref[group * 4 + j]
-        q = jnp.concatenate([q_ref[2 * j], q_ref[2 * j + 1]], axis=1)
-        scores = jnp.where(valid, mm(q, k_ref[j], NT) * SCALE, NEG)
+    lengths = len_ref[...]
+    for r in range(16):
+        valid = places < lengths[:, r : r + 1]
+        q = jnp.concatenate([q_ref[2 * r], q_ref[2 * r + 1]], axis=1)
+        scores = jnp.where(valid, mm(q, k_ref[r], NT) * SCALE, NEG)
         top = jnp.max(scores, axis=1, keepdims=True)
         weights = jnp.where(valid, jnp.exp(scores - top), 0.0)
         mass = jnp.sum(weights, axis=1, keepdims=True)
-        acc = mm(weights.astype(BF), v_ref[j])
+        acc = mm(weights.astype(BF), v_ref[r])
         stats = jnp.where(lane < 64, top, mass)
-        out_ref[2 * j] = jnp.where(row < 4, acc[:, :128], pltpu.roll(stats, 4, 0))
-        out_ref[2 * j + 1] = jnp.where(row < 4, pltpu.roll(acc[:, 128:], 4, 0), stats)
+        out_ref[2 * r] = jnp.where(row < 4, acc[:, :128], pltpu.roll(stats, 4, 0))
+        out_ref[2 * r + 1] = jnp.where(row < 4, pltpu.roll(acc[:, 128:], 4, 0), stats)
 
 
 def combine_kernel(got_ref, new_ref, out_ref):
@@ -245,34 +267,44 @@
     return lax.all_to_all(values, axis, 0, 0, tiled=False)
 
 
+def angle_tables():
+    freq = 10000.0 ** (-2.0 * np.arange(64) / HD)
+    tables = []
+    for positions in (np.arange(136) * 128, np.arange(128)):
+        angles = positions[:, None] * freq[None, :]
+        tables.append(np.concatenate([np.cos(angles), np.sin(angles)], axis=1).astype(np.float32))
+    return tables
+
+
 def per_device(
     tokens, attn_in_weight, attn_out_weight, ffn_in_weight, ffn_out_weight, cache_keys, cache_values, lengths
 ):
     x = tokens.reshape(64, 64)
-    place = lax.axis_index("seq")
-    freq = (10000.0 ** (-2.0 * np.arange(64) / HD)).astype(np.float32)
-    freq = jnp.asarray(np.concatenate([freq, freq]))
-    length = lax.dynamic_slice(lengths, (place // 2,), (1,))
-    angles = (length + jnp.arange(4, dtype=jnp.int32)).astype(F32)[:, None] * freq[None, :]
-    sign = jnp.asarray(np.concatenate([-np.ones(64, np.float32), np.ones(64, np.float32)]))
-    cos, sin = jnp.cos(angles), jnp.sin(angles) * sign[None, :]
-
-    got = exchange(call(qkv_kernel, 2, ((32, 4, 512), F32))(x, attn_in_weight), "seq")
-    queries, new = call(rope_kernel, 3, ((32, 8, 128), BF), ((8, 128), F32))(got, cos, sin)
+    coarse, fine = (jnp.asarray(table) for table in angle_tables())
+    part = pl.pallas_call(
+        qkv_kernel,
+        out_shape=jax.ShapeDtypeStruct((32, 4, 512), F32),
+        in_specs=[pl.BlockSpec(memory_space=pl.ANY)] * 2,
+        out_specs=VM,
+        scratch_shapes=[
+            pltpu.VMEM((64, 64), BF),
+            pltpu.VMEM((3, 64, 256), BF),
+            pltpu.SemaphoreType.DMA((2,)),
+        ],
+        compiler_params=pltpu.CompilerParams(vmem_limit_bytes=60 << 20),
+        cost_estimate=LONG,
+    )(x, attn_in_weight)
+    got = exchange(part, "seq")
+    queries, new = pl.pallas_call(
+        rope_kernel,
+        out_shape=[jax.ShapeDtypeStruct((32, 8, 128), BF), jax.ShapeDtypeStruct((8, 128), F32)],
+        in_specs=[pl.BlockSpec(memory_space=pltpu.SMEM)] + [VM] * 3,
+        out_specs=[VM] * 2,
+        compiler_params=PARAMS,
+        cost_estimate=LONG,
+    )(lengths, got, coarse, fine)
     queries = exchange(queries, "seq")
-    blocks = pl.pallas_call(
-        attend_kernel,
-        out_shape=jax.ShapeDtypeStruct((32, 8, 128), F32),
-        grid=(4,),
-        in_specs=[
-            pl.BlockSpec(memory_space=pltpu.SMEM),
-            pl.BlockSpec((8, 8, 128), lambda g: (g, 0, 0)),
-            pl.BlockSpec((4, 512, 256), lambda g: (g, 0, 0)),
-            pl.BlockSpec((4, 512, 256), lambda g: (g, 0, 0)),
-        ],
-        out_specs=pl.BlockSpec((8, 8, 128), lambda g: (g, 0, 0)),
-        compiler_params=pltpu.CompilerParams(vmem_limit_bytes=24 << 20),
-    )(lengths, queries, cache_keys, cache_values)
+    blocks = call(attend_kernel, 4, ((32, 8, 128), F32))(lengths.reshape(1, 16), queries, cache_keys, cache_values)
     attended = exchange(call(combine_kernel, 2, ((32, 8, 128), BF))(exchange(blocks, "seq"), new), "seq")
     part = call(out_proj_kernel, 2, ((8, 32, 128), F32))(attended, attn_out_weight.T)
     branch, part = call(ffn_in_kernel, 3, ((64, 64), BF), ((32, 40, 128), BF))(

time: 134 us -> 128 us (0.955)
  blocking collectives: 92.6 us -> 116 us
  starting transfers between devices: 12 us -> 0 us
  waiting for transfers between devices: 8.49 us -> 0 us
  local copies, waits for them, and re-layouts: 7.89 us -> 0.05 us
  other arithmetic: 1.43 us -> 0 us
    all_to_all x7 -> x8, blocking collectives: 92.6 us -> 116 us  [exchange(): return lax.all_to_all(values, axis, 0, 0, tiled=False)]
    all_to_all x1 -> x0, starting transfers between devices: 12 us -> none  [exchange(): return lax.all_to_all(values, axis, 0, 0, tiled=False)]
    all_to_all x1 -> x0, waiting for transfers between devices: 8.49 us -> none  [exchange(): return lax.all_to_all(values, axis, 0, 0, tiled=False)]
    unnamed x18, local copies, waits for them, and re-layouts: 6.65 us -> 0.05 us
  transfers between devices with their start and end apart: 1 -> 0, of which waited for: 1 -> 0; matrix products, arithmetic and copies ran while one was open for 2% -> 0% of each run, Pallas kernels for 0% -> 0%
where the time goes in v2:
time: 128 us
  blocking collectives  116 us (91%)
  Pallas kernels  10.9 us (9%)
    all_to_all x8, blocking collectives, exchange(): return lax.all_to_all(values, axis, 0, 0, tiled=False)  116 us
    pallas_call x1, Pallas kernels, per_device(): call(attend_kernel, 4, ((32, 8, 128), F32))  5.01 us

profile of v2, /device:TPU:1, one launch (start us, length us, event | category | flops | bytes accessed | tf_op | source)
XLA Modules:
  0.0 127.8 jit_solution(13174138423075410557)
XLA Ops:
  0.6 0.0 copy-start.6
  0.6 0.0 copy-start.7
  0.7 0.0 copy-start.8
  0.7 2.1 %shard_map.113 = f32[32,4,512]{2,1,0:T(4,128)} custom-call(bf16[64,64]{1,0:T(8,128)(2,1)} %bitcast.8, bf16[3,64,256]{2,1,0:T(8,128)(2,1)} %w_hbm.1), custom_call_target="tpu_custom_call" | custom-call | flops 1099511627776 | bytes 1099511627776 | tf_op jit(solution)/shard_map/pallas_call | solution.py:284
  2.8 23.2 %all_to_all.40.got_ref = f32[32,4,512]{2,1,0:T(4,128)S(1)} all-to-all(f32[32,4,512]{2,1,0:T(4,128)} %shard_map.113), channel_id=1, replica_groups=mesh['head'=8,'seq'=32] {'seq'}, dimensions={0} | all-to-all | bytes 524288 | tf_op jit(solution)/shard_map/all_to_all | solution.py:267
  26.0 0.0 copy-done.6
  26.0 0.0 copy-done.7
  26.0 0.0 copy-done.8
  26.1 0.0 copy-start
  26.1 0.0 copy-start.1
  26.1 0.8 shard_map.114
  26.9 13.6 %all_to_all.41.q_ref = bf16[32,8,128]{2,1,0:T(8,128)(2,1)S(1)} all-to-all(bf16[32,8,128]{2,1,0:T(8,128)(2,1)S(1)} %get-tuple-element.6), channel_id=1, replica_groups=mesh['head'=8,'seq'=32] {'seq'}, dimensions={0} | all-to-all | bytes 131072 | tf_op jit(solution)/shard_map/all_to_all | solution.py:267
  40.6 0.0 copy-done
  40.6 0.0 copy-done.1
  40.6 0.0 copy-start.4
  40.6 0.0 copy-start.2
  40.6 0.0 copy-start.5
  40.6 0.0 copy-start.3
  40.6 5.0 %shard_map.115 = f32[32,8,128]{2,1,0:T(8,128)S(1)} custom-call(s32[1,16]{1,0:T(1,128)S(1)} %bitcast.10, bf16[32,8,128]{2,1,0:T(8,128)(2,1)S(1)} %all_to_all.41.q_ref, bf16[16,512,256]{2,1,0:T(8,128)(2,1)S(1)} %copy-done, bf16[16,512,256]{2,1,0:T(8,128)(2,1)S(1)} %copy-done.1), custom_call_target="tpu_custom_call" | custom-call | tf_op jit(solution)/shard_map/pallas_call | solution.py:307
  45.6 12.5 %all_to_all.42.got_ref = f32[32,8,128]{2,1,0:T(8,128)S(1)} all-to-all(f32[32,8,128]{2,1,0:T(8,128)S(1)} %shard_map.115), channel_id=1, replica_groups=mesh['head'=8,'seq'=32] {'seq'}, dimensions={0} | all-to-all | bytes 262144 | tf_op jit(solution)/shard_map/all_to_all | solution.py:267
  58.1 0.2 shard_map.116
  58.3 12.0 %all_to_all.43.got_ref = bf16[32,8,128]{2,1,0:T(8,128)(2,1)S(1)} all-to-all(bf16[32,8,128]{2,1,0:T(8,128)(2,1)S(1)} %shard_map.116), channel_id=1, replica_groups=mesh['head'=8,'seq'=32] {'seq'}, dimensions={0} | all-to-all | bytes 131072 | tf_op jit(solution)/shard_map/all_to_all | solution.py:267
  70.3 0.0 copy-done.4
  70.3 0.2 shard_map.117
  70.5 14.6 %all_to_all.44.got_ref = f32[8,32,128]{2,1,0:T(8,128)S(1)} all-to-all(f32[8,32,128]{2,1,0:T(8,128)S(1)} %shard_map.117), channel_id=1, replica_groups=mesh['head'=8,'seq'=32] {'head'}, dimensions={0} | all-to-all | bytes 262144 | tf_op jit(solution)/shard_map/all_to_all | solution.py:267
  85.1 0.0 copy-done.2
  85.1 0.0 copy-done.5
  85.1 1.0 shard_map.118
  86.1 15.5 %all_to_all.45.got_ref = bf16[32,40,128]{2,1,0:T(8,128)(2,1)S(1)} all-to-all(bf16[32,40,128]{2,1,0:T(8,128)(2,1)S(1)} %get-tuple-element.9), channel_id=1, replica_groups=mesh['head'=8,'seq'=32] {'seq'}, dimensions={0} | all-to-all | bytes 655360 | tf_op jit(solution)/shard_map/all_to_all | solution.py:267
  101.6 0.4 shard_map.119
  102.1 13.8 %all_to_all.46.got_ref = bf16[32,16,128]{2,1,0:T(8,128)(2,1)S(1)} all-to-all(bf16[32,16,128]{2,1,0:T(8,128)(2,1)S(1)} %shard_map.119), channel_id=1, replica_groups=mesh['head'=8,'seq'=32] {'seq'}, dimensions={0} | all-to-all | bytes 262144 | tf_op jit(solution)/shard_map/all_to_all | solution.py:267
  115.9 0.0 copy-done.3
  115.9 0.3 shard_map.120
  116.2 10.8 %all_to_all.47.got_ref = f32[8,32,128]{2,1,0:T(8,128)S(1)} all-to-all(f32[8,32,128]{2,1,0:T(8,128)S(1)} %shard_map.120), channel_id=1, replica_groups=mesh['head'=8,'seq'=32] {'head'}, dimensions={0} | all-to-all | bytes 262144 | tf_op jit(solution)/shard_map/all_to_all | solution.py:267
  127.0 0.8 shard_map.121
Async XLA Ops:
  0.6 25.4 %copy-start.6 = (s32[16]{0:T(128)S(1)}, s32[16]{0:T(128)}, u32[]{:S(2)}) copy-start(s32[16]{0:T(128)} %len_ref.1) | copy-start | bytes 196
  0.6 25.4 %copy-start.7 = (f32[136,128]{1,0:T(8,128)S(1)}, f32[136,128]{1,0:T(8,128)}, u32[]{:S(2)}) copy-start(f32[136,128]{1,0:T(8,128)} %constant.4.clone.coarse_ref) | copy-start | bytes 208900
  0.7 25.4 %copy-start.8 = (f32[128,128]{1,0:T(8,128)S(1)}, f32[128,128]{1,0:T(8,128)}, u32[]{:S(2)}) copy-start(f32[128,128]{1,0:T(8,128)} %constant.5.clone.fine_ref) | copy-start | bytes 196612
  26.1 14.5 %copy-start = (bf16[16,512,256]{2,1,0:T(8,128)(2,1)S(1)}, bf16[16,512,256]{2,1,0:T(8,128)(2,1)}, u32[]{:S(2)}) copy-start(bf16[16,512,256]{2,1,0:T(8,128)(2,1)} %k_ref.1) | copy-start | bytes 12582916
  26.1 14.5 %copy-start.1 = (bf16[16,512,256]{2,1,0:T(8,128)(2,1)S(1)}, bf16[16,512,256]{2,1,0:T(8,128)(2,1)}, u32[]{:S(2)}) copy-start(bf16[16,512,256]{2,1,0:T(8,128)(2,1)} %v_ref.1) | copy-start | bytes 12582916
  40.6 29.7 %copy-start.4 = (bf16[256,64]{0,1:T(8,128)(2,1)S(1)}, bf16[256,64]{0,1:T(8,128)(2,1)}, u32[]{:S(2)}) copy-start(bf16[256,64]{0,1:T(8,128)(2,1)} %param.12) | copy-start | bytes 98308
  40.6 44.5 %copy-start.2 = (bf16[2,64,1024]{2,1,0:T(8,128)(2,1)S(1)}, bf16[2,64,1024]{2,1,0:T(8,128)(2,1)}, u32[]{:S(2)}) copy-start(bf16[2,64,1024]{2,1,0:T(8,128)(2,1)} %w_ref.1) | copy-start | bytes 786436
  40.6 44.5 %copy-start.5 = (bf16[4,16,64]{2,1,0:T(8,128)(2,1)S(1)}, bf16[4,16,64]{2,1,0:T(8,128)(2,1)}, u32[]{:S(2)}) copy-start(bf16[4,16,64]{2,1,0:T(8,128)(2,1)} %param.10) | copy-start | bytes 24580
  40.6 75.3 %copy-start.3 = (bf16[1024,64]{0,1:T(8,128)(2,1)S(1)}, bf16[1024,64]{0,1:T(8,128)(2,1)}, u32[]{:S(2)}) copy-start(bf16[1024,64]{0,1:T(8,128)(2,1)} %param.14) | copy-start | bytes 393220

commit v3 on v2

--- a/solution.py
+++ b/solution.py
@@ -130,20 +130,25 @@
     new_ref[4:8, :] = jnp.where(lane < 64, top, mass)
 
 
-def attend_kernel(len_ref, q_ref, k_ref, v_ref, out_ref):
+def attend_kernel(len_ref, q_ref, k_ref, v_ref, out_ref, score_ref, weight_ref, stat_ref):
     first = lax.axis_index("seq") * 512
     places = first + iota((8, 512), 1)
     row, lane = iota((8, 128), 0), iota((8, 128), 1)
     lengths = len_ref[...]
     for r in range(16):
+        q = jnp.concatenate([q_ref[2 * r], q_ref[2 * r + 1]], axis=1)
+        score_ref[r] = mm(q, k_ref[r], NT) * SCALE
+    for r in range(16):
         valid = places < lengths[:, r : r + 1]
-        q = jnp.concatenate([q_ref[2 * r], q_ref[2 * r + 1]], axis=1)
-        scores = jnp.where(valid, mm(q, k_ref[r], NT) * SCALE, NEG)
+        scores = jnp.where(valid, score_ref[r], NEG)
         top = jnp.max(scores, axis=1, keepdims=True)
         weights = jnp.where(valid, jnp.exp(scores - top), 0.0)
         mass = jnp.sum(weights, axis=1, keepdims=True)
-        acc = mm(weights.astype(BF), v_ref[r])
-        stats = jnp.where(lane < 64, top, mass)
+        weight_ref[r] = weights.astype(BF)
+        stat_ref[r] = jnp.where(lane < 64, top, mass)
+    for r in range(16):
+        acc = mm(weight_ref[r], v_ref[r])
+        stats = stat_ref[r]
         out_ref[2 * r] = jnp.where(row < 4, acc[:, :128], pltpu.roll(stats, 4, 0))
         out_ref[2 * r + 1] = jnp.where(row < 4, pltpu.roll(acc[:, 128:], 4, 0), stats)
 
@@ -183,11 +188,11 @@
     rows = got[:, 0] + got[:, 1]
     attended = jnp.concatenate([rows[:, 0].reshape(64, 128), rows[:, 1].reshape(64, 128)], axis=1).astype(BF)
     part = mm(w_ref[...], attended, NT)
-    out_ref[...] = jnp.broadcast_to(pack(part)[None], (8, 32, 128))
+    out_ref[...] = jnp.broadcast_to(pack(part).astype(BF)[None], (8, 32, 128))
 
 
 def ffn_in_kernel(got_ref, x_ref, w_ref, branch_ref, out_ref):
-    branch = unpack(jnp.sum(got_ref[...], axis=0))
+    branch = unpack(jnp.sum(got_ref[...].astype(F32), axis=0))
     branch_ref[...] = mm(to_step_major(), branch.astype(BF), NT).astype(BF)
     eye = one_hot(iota((64, 64), 0) == iota((64, 64), 1))
     xt = mm(eye, mm(to_request_major(), x_ref[...]).astype(BF), NT)
@@ -243,15 +248,15 @@
     low = mm(w_ref[:, 0:512], hidden)
     high = mm(w_ref[:, 512:1024], hidden)
     part = low[:, 0:64] + high[:, 64:128]
-    out_ref[...] = jnp.broadcast_to(pack(part)[None], (8, 32, 128))
+    out_ref[...] = jnp.broadcast_to(pack(part).astype(BF)[None], (8, 32, 128))
 
 
 def final_kernel(got_ref, out_ref):
-    total = unpack(jnp.sum(got_ref[...], axis=0))
+    total = unpack(jnp.sum(got_ref[...].astype(F32), axis=0))
     out_ref[...] = mm(to_step_major(), total.astype(BF), NT).astype(BF)
 
 
-def call(kernel, n_in, *outs):
+def call(kernel, n_in, *outs, scratch=()):
     shapes = [jax.ShapeDtypeStruct(shape, dtype) for shape, dtype in outs]
     one = len(shapes) == 1
     return pl.pallas_call(
@@ -259,6 +264,7 @@
         out_shape=shapes[0] if one else shapes,
         in_specs=[VM] * n_in,
         out_specs=VM if one else [VM] * len(shapes),
+        scratch_shapes=scratch,
         compiler_params=PARAMS,
     )
 
@@ -284,16 +290,19 @@
     part = pl.pallas_call(
         qkv_kernel,
         out_shape=jax.ShapeDtypeStruct((32, 4, 512), F32),
-        in_specs=[pl.BlockSpec(memory_space=pl.ANY)] * 2,
+        in_specs=[pl.BlockSpec(memory_space=pltpu.HBM)] * 2,
         out_specs=VM,
         scratch_shapes=[
             pltpu.VMEM((64, 64), BF),
             pltpu.VMEM((3, 64, 256), BF),
             pltpu.SemaphoreType.DMA((2,)),
         ],
-        compiler_params=pltpu.CompilerParams(vmem_limit_bytes=60 << 20),
+        compiler_params=PARAMS,
         cost_estimate=LONG,
-    )(x, attn_in_weight)
+    )(
+        pltpu.with_memory_space_constraint(x, pltpu.HBM),
+        pltpu.with_memory_space_constraint(attn_in_weight, pltpu.HBM),
+    )
     got = exchange(part, "seq")
     queries, new = pl.pallas_call(
         rope_kernel,
@@ -304,14 +313,15 @@
         cost_estimate=LONG,
     )(lengths, got, coarse, fine)
     queries = exchange(queries, "seq")
-    blocks = call(attend_kernel, 4, ((32, 8, 128), F32))(lengths.reshape(1, 16), queries, cache_keys, cache_values)
+    scratch = [pltpu.VMEM((16, 8, 512), F32), pltpu.VMEM((16, 8, 512), BF), pltpu.VMEM((16, 8, 128), F32)]
+    blocks = call(attend_kernel, 4, ((32, 8, 128), F32), scratch=scratch)(lengths.reshape(1, 16), queries, cache_keys, cache_values)
     attended = exchange(call(combine_kernel, 2, ((32, 8, 128), BF))(exchange(blocks, "seq"), new), "seq")
-    part = call(out_proj_kernel, 2, ((8, 32, 128), F32))(attended, attn_out_weight.T)
+    part = call(out_proj_kernel, 2, ((8, 32, 128), BF))(attended, attn_out_weight.T)
     branch, part = call(ffn_in_kernel, 3, ((64, 64), BF), ((32, 40, 128), BF))(
         exchange(part, "head"), x, ffn_in_weight
     )
     hidden = exchange(call(hidden_kernel, 1, ((32, 16, 128), BF))(exchange(part, "seq")), "seq")
-    part = call(ffn_out_kernel, 2, ((8, 32, 128), F32))(hidden, ffn_out_weight.T)
+    part = call(ffn_out_kernel, 2, ((8, 32, 128), BF))(hidden, ffn_out_weight.T)
     mlp = call(final_kernel, 1, ((64, 64), BF))(exchange(part, "head"))
     return branch.reshape(4, 16, 64), mlp.reshape(4, 16, 64)
 

time: 128 us -> 123 us (0.961)
  Pallas kernels: 10.9 us -> 6.99 us
    pallas_call x3, Pallas kernels: 5.52 us -> 2.33 us  [the longest x1 1.82 us: per_device(): call(attend_kernel, 4, ((32, 8, 128), F32), scratch=scratch)]
where the time goes in v3:
time: 123 us
  blocking collectives  115 us (93%)
  Pallas kernels  6.99 us (6%)
    all_to_all x8, blocking collectives, exchange(): return lax.all_to_all(values, axis, 0, 0, tiled=False)  115 us

profile of v3, /device:TPU:1, one launch (start us, length us, event | category | flops | bytes accessed | tf_op | source)
XLA Modules:
  0.0 122.8 jit_solution(894010738581256699)
XLA Ops:
  0.6 0.0 copy-start.6
  0.6 0.0 copy-start.7
  0.7 0.0 copy-start.8
  0.7 1.4 %shard_map.113 = f32[32,4,512]{2,1,0:T(4,128)S(1)} custom-call(bf16[64,64]{1,0:T(8,128)(2,1)} %bitcast.8, bf16[3,64,256]{2,1,0:T(8,128)(2,1)} %w_hbm.1), custom_call_target="tpu_custom_call" | custom-call | flops 1099511627776 | bytes 1099511627776 | tf_op jit(solution)/shard_map/pallas_call | solution.py:290
  2.1 23.0 %all_to_all.40.got_ref = f32[32,4,512]{2,1,0:T(4,128)S(1)} all-to-all(f32[32,4,512]{2,1,0:T(4,128)S(1)} %shard_map.113), channel_id=1, replica_groups=mesh['head'=8,'seq'=32] {'seq'}, dimensions={0} | all-to-all | bytes 524288 | tf_op jit(solution)/shard_map/all_to_all | solution.py:273
  25.1 0.0 copy-done.6
  25.1 0.0 copy-done.7
  25.1 0.0 copy-done.8
  25.1 0.0 copy-start
  25.1 0.0 copy-start.1
  25.2 0.8 shard_map.114
  26.0 13.6 %all_to_all.41.q_ref = bf16[32,8,128]{2,1,0:T(8,128)(2,1)S(1)} all-to-all(bf16[32,8,128]{2,1,0:T(8,128)(2,1)S(1)} %get-tuple-element.6), channel_id=1, replica_groups=mesh['head'=8,'seq'=32] {'seq'}, dimensions={0} | all-to-all | bytes 131072 | tf_op jit(solution)/shard_map/all_to_all | solution.py:273
  39.6 0.0 copy-done
  39.6 0.0 copy-done.1
  39.6 0.0 copy-start.4
  39.6 0.0 copy-start.2
  39.7 0.0 copy-start.5
  39.7 0.0 copy-start.3
  39.7 1.8 %shard_map.115 = f32[32,8,128]{2,1,0:T(8,128)S(1)} custom-call(s32[1,16]{1,0:T(1,128)S(1)} %bitcast.10, bf16[32,8,128]{2,1,0:T(8,128)(2,1)S(1)} %all_to_all.41.q_ref, bf16[16,512,256]{2,1,0:T(8,128)(2,1)S(1)} %copy-done, bf16[16,512,256]{2,1,0:T(8,128)(2,1)S(1)} %copy-done.1), custom_call_target="tpu_custom_call" | custom-call | tf_op jit(solution)/shard_map/pallas_call | solution.py:317
  41.5 12.5 %all_to_all.42.got_ref = f32[32,8,128]{2,1,0:T(8,128)S(1)} all-to-all(f32[32,8,128]{2,1,0:T(8,128)S(1)} %shard_map.115), channel_id=1, replica_groups=mesh['head'=8,'seq'=32] {'seq'}, dimensions={0} | all-to-all | bytes 262144 | tf_op jit(solution)/shard_map/all_to_all | solution.py:273
  54.0 0.2 shard_map.116
  54.1 12.0 %all_to_all.43.got_ref = bf16[32,8,128]{2,1,0:T(8,128)(2,1)S(1)} all-to-all(bf16[32,8,128]{2,1,0:T(8,128)(2,1)S(1)} %shard_map.116), channel_id=1, replica_groups=mesh['head'=8,'seq'=32] {'seq'}, dimensions={0} | all-to-all | bytes 131072 | tf_op jit(solution)/shard_map/all_to_all | solution.py:273
  66.1 0.0 copy-done.4
  66.2 0.2 shard_map.117
  66.4 14.2 %all_to_all.44.got_ref = bf16[8,32,128]{2,1,0:T(8,128)(2,1)S(1)} all-to-all(bf16[8,32,128]{2,1,0:T(8,128)(2,1)S(1)} %shard_map.117), channel_id=1, replica_groups=mesh['head'=8,'seq'=32] {'head'}, dimensions={0} | all-to-all | bytes 131072 | tf_op jit(solution)/shard_map/all_to_all | solution.py:273
  80.5 0.0 copy-done.2
  80.5 0.0 copy-done.5
  80.5 1.0 shard_map.118
  81.5 15.7 %all_to_all.45.got_ref = bf16[32,40,128]{2,1,0:T(8,128)(2,1)S(1)} all-to-all(bf16[32,40,128]{2,1,0:T(8,128)(2,1)S(1)} %get-tuple-element.9), channel_id=1, replica_groups=mesh['head'=8,'seq'=32] {'seq'}, dimensions={0} | all-to-all | bytes 655360 | tf_op jit(solution)/shard_map/all_to_all | solution.py:273
  97.2 0.4 shard_map.119
  97.6 13.8 %all_to_all.46.got_ref = bf16[32,16,128]{2,1,0:T(8,128)(2,1)S(1)} all-to-all(bf16[32,16,128]{2,1,0:T(8,128)(2,1)S(1)} %shard_map.119), channel_id=1, replica_groups=mesh['head'=8,'seq'=32] {'seq'}, dimensions={0} | all-to-all | bytes 262144 | tf_op jit(solution)/shard_map/all_to_all | solution.py:273
  111.4 0.0 copy-done.3
  111.4 0.3 shard_map.120
  111.7 10.3 %all_to_all.47.got_ref = bf16[8,32,128]{2,1,0:T(8,128)(2,1)S(1)} all-to-all(bf16[8,32,128]{2,1,0:T(8,128)(2,1)S(1)} %shard_map.120), channel_id=1, replica_groups=mesh['head'=8,'seq'=32] {'head'}, dimensions={0} | all-to-all | bytes 131072 | tf_op jit(solution)/shard_map/all_to_all | solution.py:273
  122.0 0.8 shard_map.121
Async XLA Ops:
  0.6 24.5 %copy-start.6 = (s32[16]{0:T(128)S(1)}, s32[16]{0:T(128)}, u32[]{:S(2)}) copy-start(s32[16]{0:T(128)} %len_ref.1) | copy-start | bytes 196
  0.6 24.5 %copy-start.7 = (f32[136,128]{1,0:T(8,128)S(1)}, f32[136,128]{1,0:T(8,128)}, u32[]{:S(2)}) copy-start(f32[136,128]{1,0:T(8,128)} %constant.4.clone.coarse_ref) | copy-start | bytes 208900
  0.7 24.5 %copy-start.8 = (f32[128,128]{1,0:T(8,128)S(1)}, f32[128,128]{1,0:T(8,128)}, u32[]{:S(2)}) copy-start(f32[128,128]{1,0:T(8,128)} %constant.5.clone.fine_ref) | copy-start | bytes 196612
  25.1 14.5 %copy-start = (bf16[16,512,256]{2,1,0:T(8,128)(2,1)S(1)}, bf16[16,512,256]{2,1,0:T(8,128)(2,1)}, u32[]{:S(2)}) copy-start(bf16[16,512,256]{2,1,0:T(8,128)(2,1)} %k_ref.1) | copy-start | bytes 12582916
  25.1 14.5 %copy-start.1 = (bf16[16,512,256]{2,1,0:T(8,128)(2,1)S(1)}, bf16[16,512,256]{2,1,0:T(8,128)(2,1)}, u32[]{:S(2)}) copy-start(bf16[16,512,256]{2,1,0:T(8,128)(2,1)} %v_ref.1) | copy-start | bytes 12582916
  39.6 26.5 %copy-start.4 = (bf16[256,64]{0,1:T(8,128)(2,1)S(1)}, bf16[256,64]{0,1:T(8,128)(2,1)}, u32[]{:S(2)}) copy-start(bf16[256,64]{0,1:T(8,128)(2,1)} %param.12) | copy-start | bytes 98308
  39.6 40.9 %copy-start.2 = (bf16[2,64,1024]{2,1,0:T(8,128)(2,1)S(1)}, bf16[2,64,1024]{2,1,0:T(8,128)(2,1)}, u32[]{:S(2)}) copy-start(bf16[2,64,1024]{2,1,0:T(8,128)(2,1)} %w_ref.1) | copy-start | bytes 786436
  39.7 40.9 %copy-start.5 = (bf16[4,16,64]{2,1,0:T(8,128)(2,1)S(1)}, bf16[4,16,64]{2,1,0:T(8,128)(2,1)}, u32[]{:S(2)}) copy-start(bf16[4,16,64]{2,1,0:T(8,128)(2,1)} %param.10) | copy-start | bytes 24580
  39.7 71.7 %copy-start.3 = (bf16[1024,64]{0,1:T(8,128)(2,1)S(1)}, bf16[1024,64]{0,1:T(8,128)(2,1)}, u32[]{:S(2)}) copy-start(bf16[1024,64]{0,1:T(8,128)(2,1)} %param.14) | copy-start | bytes 393220
